TPU v7x, 32 devices: a whole 2x2x4 slice. The times are simulated.
32 devices in a mesh: region: 8 (over z, core), head: 4 (over y, x).
Axes of the slice: x: 2, y: 2, z: 4, core: 2. Of those that a mesh axis runs over, the one named last changes fastest.
Arguments:
- fine_tokens: float32 [18432, 512], P(('region', 'head')), may hold values from -6 to 6
- fine_shift: int32 [1], replicated, may hold values from 1 to 143
- window_counts: int32 [32], P('region'), may hold values from 36 to 144
- fine_qkv: bfloat16 [512, 1536], replicated, may hold values from -4 to 4
- fine_proj: bfloat16 [512, 512], replicated, may hold values from -0.25 to 0.25
- fine_up: bfloat16 [512, 2048], replicated, may hold values from -0.25 to 0.25
- fine_down: bfloat16 [2048, 512], replicated, may hold values from -0.125 to 0.125
- merge_weight: bfloat16 [2048, 1024], replicated, may hold values from -0.125 to 0.125
- coarse_qkv: bfloat16 [1024, 3072], P('region', 'head'), may hold values from -4 to 4
- coarse_proj: bfloat16 [1024, 1024], P('head', 'region'), may hold values from -0.1875 to 0.1875
- coarse_up: bfloat16 [1024, 4096], P('region', 'head'), may hold values from -0.1875 to 0.1875
- coarse_down: bfloat16 [4096, 1024], P('head', 'region'), may hold values from -0.09375 to 0.09375
- expand_weight: bfloat16 [1024, 2048], replicated, may hold values from -0.1875 to 0.1875
- out_weight: bfloat16 [1024, 512], replicated, may hold values from -0.1875 to 0.1875
Outputs:
- fine_result: float32 [18432, 512], P(('region', 'head'))
All inputs are finite; a program needn't handle non-finite values.
Results may differ from a plain program's by a relative error of at most 0.012.
Values may be sent and summed in bfloat16 or wider, within the bound.
A program may use at most 128 MiB of HBM per device.

v0:
```python
import jax
import jax.numpy as jnp
from jax import lax
from jax.sharding import PartitionSpec as P

C = 512
HD = 64
HF = 8
WIN = 144


def shifted(value, axis, steps):
    count = lax.axis_size(axis)
    pairs = [(source, (source + steps) % count) for source in range(count)]
    return lax.ppermute(value, axis, pairs)


def layer_norm(values):
    average = jnp.mean(values, axis=-1, keepdims=True)
    centred = values - average
    spread = jnp.mean(centred * centred, axis=-1, keepdims=True)
    return centred * lax.rsqrt(spread + 1e-05)


def window_attention(normed, qkv_weight, proj_weight, head_count, head_size, window, counts):
    row_count = normed.shape[0]
    window_total = row_count // window
    weight_heads = qkv_weight.reshape(qkv_weight.shape[0], head_count, 3 * head_size)
    packed = jnp.einsum(
        "nc,chj->hnj", normed, weight_heads, preferred_element_type=jnp.float32
    ).astype(jnp.bfloat16)
    packed = packed.reshape(head_count, window_total, window, 3 * head_size)
    queries = packed[..., :head_size]
    key_part = packed[..., head_size : 2 * head_size]
    value_part = packed[..., 2 * head_size :]
    scores = jnp.einsum(
        "hwqd,hwkd->hwqk", queries, key_part, preferred_element_type=jnp.float32
    ) * head_size ** (-0.5)
    if counts is not None:
        position = jnp.arange(window, dtype=jnp.int32)
        visible = position[None, :] < counts[:, None]
        scores = jnp.where(visible[None, :, None, :], scores, -1e30)
    row_max = jnp.max(scores, axis=-1, keepdims=True)
    raised = jnp.exp(scores - row_max)
    weights = (raised / jnp.sum(raised, axis=-1, keepdims=True)).astype(jnp.bfloat16)
    blended = jnp.einsum(
        "hwqk,hwkd->hwqd", weights, value_part, preferred_element_type=jnp.float32
    ).astype(jnp.bfloat16)
    blended = blended.reshape(head_count, row_count, head_size)
    proj_heads = proj_weight.reshape(head_count, head_size, proj_weight.shape[1])
    return jnp.einsum("hnd,hdc->nc", blended, proj_heads, preferred_element_type=jnp.float32)


def hidden_layer(normed, up_weight):
    hidden = jnp.dot(normed, up_weight, preferred_element_type=jnp.float32)
    return jax.nn.gelu(hidden, approximate=False).astype(jnp.bfloat16)


def body(
    fine_tokens,
    fine_shift,
    window_counts,
    fine_qkv,
    fine_proj,
    fine_up,
    fine_down,
    merge_weight,
    coarse_qkv,
    coarse_proj,
    coarse_up,
    coarse_down,
    expand_weight,
    out_weight,
):
    offset = fine_shift[0]
    local_rows = fine_tokens.shape[0]
    normed = layer_norm(fine_tokens).astype(jnp.bfloat16)
    following = shifted(normed[:WIN], ("region", "head"), -1)
    extended = jnp.concatenate([normed, following], axis=0)
    rolled = lax.dynamic_slice_in_dim(extended, offset, local_rows, 0)
    attended = window_attention(rolled, fine_qkv, fine_proj, HF, HD, WIN, None)
    placed = lax.dynamic_update_slice_in_dim(
        jnp.zeros((local_rows + WIN, C), jnp.float32), attended, offset, 0
    )
    arrived = shifted(placed[local_rows:].astype(jnp.bfloat16), ("region", "head"), 1).astype(
        jnp.float32
    )
    restored = placed[:local_rows].at[:WIN].add(arrived)
    fine_mid = fine_tokens + restored
    fine_hidden = hidden_layer(layer_norm(fine_mid).astype(jnp.bfloat16), fine_up)
    fine_out = fine_mid + jnp.dot(fine_hidden, fine_down, preferred_element_type=jnp.float32)
    merged = fine_out.reshape(local_rows // 4, 4 * C)
    grouped = layer_norm(merged).astype(jnp.bfloat16)
    coarse = jnp.dot(grouped, merge_weight, preferred_element_type=jnp.float32)
    coarse_norm = layer_norm(coarse).astype(jnp.bfloat16)
    weight_parts = (coarse_qkv, coarse_proj, coarse_up, coarse_down)
    qkv_part, proj_part, up_part, down_part = (
        lax.all_gather(weight_parts[0], "region", axis=0, tiled=True),
        lax.all_gather(weight_parts[1], "region", axis=1, tiled=True),
        lax.all_gather(weight_parts[2], "region", axis=0, tiled=True),
        lax.all_gather(weight_parts[3], "region", axis=1, tiled=True),
    )
    gathered = lax.all_gather(coarse_norm, "head", axis=0, tiled=True)
    own_heads = qkv_part.shape[1] // (3 * HD)
    partial_value = window_attention(
        gathered, qkv_part, proj_part, own_heads, HD, WIN, window_counts
    )
    coarse_mid = coarse + lax.psum_scatter(
        partial_value.astype(jnp.bfloat16), "head", scatter_dimension=0, tiled=True
    ).astype(jnp.float32)
    mid_norm = layer_norm(coarse_mid).astype(jnp.bfloat16)
    mid_gathered = lax.all_gather(mid_norm, "head", axis=0, tiled=True)
    coarse_hidden = hidden_layer(mid_gathered, up_part)
    mlp_terms = jnp.dot(coarse_hidden, down_part, preferred_element_type=jnp.float32)
    coarse_out = coarse_mid + lax.psum_scatter(
        mlp_terms.astype(jnp.bfloat16), "head", scatter_dimension=0, tiled=True
    ).astype(jnp.float32)
    expanded = jnp.dot(
        coarse_out.astype(jnp.bfloat16), expand_weight, preferred_element_type=jnp.float32
    ).astype(jnp.bfloat16)
    spread_rows = expanded.reshape(local_rows, C)
    joined = jnp.concatenate([fine_out.astype(jnp.bfloat16), spread_rows], axis=1)
    return jnp.dot(joined, out_weight, preferred_element_type=jnp.float32)


def solution(mesh):
    in_specs = (
        P(("region", "head"), None),
        P(),
        P("region"),
        P(),
        P(),
        P(),
        P(),
        P(),
        P("region", "head"),
        P("head", "region"),
        P("region", "head"),
        P("head", "region"),
        P(),
        P(),
    )
    out_specs = P(("region", "head"), None)
    return jax.shard_map(body, mesh=mesh, in_specs=in_specs, out_specs=out_specs, check_vma=False)
```

profile of v0, /device:TPU:0, one launch (start us, length us, event | category | flops | bytes accessed | tf_op | source)
XLA Modules:
  0.0 317.7 jit_solution(9193669464946194685)
XLA Ops:
  6.5 1.6 reduce_sum.122
  8.2 1.5 multiply_reduce_fusion.3
  11.4 6.4 %collective-permute-start = (bf16[144,512]{1,0:T(8,128)(2,1)}, bf16[144,512]{1,0:T(8,128)(2,1)S(1)}, u32[]{:S(2)}, u32[]{:S(2)}) collective-permute-start(bf16[144,512]{1,0:T(8,128)(2,1)} %slice.58), channel_id=1, source_target_pairs={{0,31},{1,0},{2,1},{3,2},{4,3},{5,4},{6,5},{7,6},{8,7},{9,8},{10,9... | collective-permute-start | bytes 442376 | tf_op jit(solution)/shard_map/ppermute | solution.py:15
  18.5 2.3 collective-permute-done
  20.8 3.2 %fusion.76 = f32[576,1536]{0,1:S(1)} fusion(bf16[512,1536]{1,0:T(8,128)(2,1)} %param.19, s32[]{:T(128)S(6)} %select_n.8, bf16[576,512]{1,0:T(8,128)(2,1)} %copy-done.6, bf16[144,512]{1,0:T(8,128)(2,1)S(1)} %collective-permute-done), kind=kOutput, calls=%fused_computation.109 | convolution fusion | flops 907149312 | bytes 6242308
  24.0 1.5 convert_bitcast_fusion
  25.5 4.2 %copy.26 = bf16[8,576,192]{2,1,0:T(8,128)(2,1)} copy(bf16[8,576,192]{1,2,0:T(8,128)(2,1)} %convert_bitcast_fusion) | data formatting | bytes 3538944 | tf_op jit(solution)/shard_map/convert_element_type | solution.py:31
  29.7 2.5 fusion.34
  32.2 4.5 %fusion.185 = (f32[8,4,144]{2,1,0:T(4,128)S(1)}, f32[8,4,144,144]{2,3,1,0:T(8,128)S(1)}) fusion(f32[8,4,144,144]{2,3,1,0:T(8,128)S(1)} %fusion.34), kind=kOutput, calls=%fused_computation.212 | output fusion | flops 2654351 | bytes 5326848 | tf_op jit(solution)/shard_map/sub | solution.py:44
  37.5 1.8 copy.31
  39.2 3.0 reshape.143
  42.2 2.8 convolution_bitcast_fusion
  46.3 4.4 %dynamic_update_slice.3 = f32[720,512]{1,0:T(8,128)} dynamic-update-slice(f32[720,512]{1,0:T(8,128)} %broadcast_in_dim.10, f32[576,512]{1,0:T(8,128)} %convolution_bitcast_fusion, s32[]{:T(128)S(6)} %select_n.8, s32[]{:T(128)} %constant.42.clone.1) | dynamic-update-slice | bytes 2359300 | tf_op jit(solution)/shard_map/dynamic_update_slice | solution.py:82
  53.5 6.6 %collective-permute-done.1 = bf16[144,512]{1,0:T(8,128)(2,1)S(1)} collective-permute-done((bf16[144,512]{1,0:T(8,128)(2,1)S(1)}, bf16[144,512]{1,0:T(8,128)(2,1)S(1)}, u32[]{:S(2)}, u32[]{:S(2)}) %collective-permute-start.1) | collective-permute-done | bytes 147488 | tf_op jit(solution)/shard_map/ppermute | solution.py:15
  62.3 14.1 %fusion.186 = (f32[576]{0:T(1024)S(1)}, f32[576,512]{1,0:T(8,128)S(1)}) fusion(f32[576,512]{1,0:T(8,128)} %copy-done.5, bf16[2048,512]{1,0:T(8,128)(2,1)S(1)} %copy-done, bf16[512,2048]{1,0:T(8,128)(2,1)} %param.21, f32[576]{0:T(1024)S(1)} %add_rsqrt_fusion, f32[576]{0:T(1024)S(1)} %broadcast_multiply_fusion), kind=kOutput, calls=%fused_computation.213 | convolution fusion | flops 2494070272 | bytes 6560512 | tf_op jit(solution)/shard_map/dot_general | solution.py:91
  78.8 3.2 fusion.187
  84.0 14.0 %all_gather.20 = bf16[256,1024]{1,0:T(8,128)(2,1)S(1)} all-gather(bf16[256,128]{1,0:T(8,128)(2,1)S(1)} %copy-done.8), channel_id=1, replica_groups=mesh['region'=8,'head'=4] {'region'}, dimensions={1}, use_global_device_ids=true | all-gather | bytes 589824 | tf_op jit(solution)/shard_map/all_gather | solution.py:99
  98.0 9.8 %all-gather.6.cloned.1.call-done = bf16[576,1024]{1,0:T(8,128)(2,1)} async-done(((bf16[144,1024]{1,0:T(8,128)(2,1)}), bf16[576,1024]{1,0:T(8,128)(2,1)}) %all-gather.6.cloned.1.call-update) | async-done | bytes 1179664 | tf_op jit(solution)/shard_map/all_gather | solution.py:103
  107.8 26.9 %all-gather.8.cloned.1.call-done = bf16[1024,768]{1,0:T(8,128)(2,1)} async-done(((bf16[128,768]{1,0:T(8,128)(2,1)}), bf16[1024,768]{1,0:T(8,128)(2,1)}) %all-gather.8.cloned.1.call-update) | async-done | bytes 1572880 | tf_op jit(solution)/shard_map/all_gather | solution.py:98
  134.7 3.2 %fusion.195 = f32[576,768]{0,1:S(1)} fusion(bf16[576,1024]{1,0:T(8,128)(2,1)} %all-gather.6.cloned.1.call-done, bf16[1024,768]{1,0:T(8,128)(2,1)} %all-gather.8.cloned.1.call-done), kind=kOutput, calls=%fused_computation.217 | convolution fusion | flops 905969664 | bytes 4521984
  139.7 2.0 convolution_convert_fusion.2
  141.7 1.4 copy.38
  143.5 1.5 bitcast_convert_fusion
  146.2 26.8 %reduce-scatter.3.cloned.1.call-done = bf16[144,1024]{1,0:T(8,128)(2,1)} async-done(((bf16[576,1024]{1,0:T(8,128)(2,1)}), bf16[144,1024]{1,0:T(8,128)(2,1)}) %reduce-scatter.3.cloned.1.call-update) | async-done | bytes 294928 | tf_op jit(solution)/shard_map/reduce_scatter | solution.py:108
  175.3 1.8 multiply_convert_fusion.9
  177.5 26.2 %all-gather.12.cloned.1.call-done = bf16[1024,1024]{1,0:T(8,128)(2,1)} async-done(((bf16[128,1024]{1,0:T(8,128)(2,1)}), bf16[1024,1024]{1,0:T(8,128)(2,1)}) %all-gather.12.cloned.1.call-update) | async-done | bytes 2097168 | tf_op jit(solution)/shard_map/all_gather | solution.py:100
  203.7 31.5 %all-gather.14.cloned.1.call-done = bf16[1024,1024]{1,0:T(8,128)(2,1)} async-done(((bf16[1024,128]{1,0:T(8,128)(2,1)}), bf16[1024,1024]{1,0:T(8,128)(2,1)}) %all-gather.14.cloned.1.call-update) | async-done | bytes 2097168 | tf_op jit(solution)/shard_map/all_gather | solution.py:101
  235.1 28.3 %all-gather.10.cloned.1.call-done = bf16[576,1024]{1,0:T(8,128)(2,1)} async-done(((bf16[144,1024]{1,0:T(8,128)(2,1)}), bf16[576,1024]{1,0:T(8,128)(2,1)}) %all-gather.10.cloned.1.call-update) | async-done | bytes 1179664 | tf_op jit(solution)/shard_map/all_gather | solution.py:112
  263.5 10.6 %convolution_convert_fusion.1 = bf16[576,1024]{1,0:T(8,128)(2,1)} fusion(bf16[1024,1024]{1,0:T(8,128)(2,1)} %all-gather.14.cloned.1.call-done, bf16[576,1024]{1,0:T(8,128)(2,1)} %all-gather.10.cloned.1.call-done, bf16[1024,1024]{1,0:T(8,128)(2,1)} %all-gather.12.cloned.1.call-done), kind=kOutput, calls=%fused_computation.54 | convolution fusion | flops 2454847488 | bytes 6553600 | tf_op jit(solution)/shard_map/dot_general | solution.py:114
  274.1 28.9 %reduce-scatter.5.cloned.1.call-done = bf16[144,1024]{1,0:T(8,128)(2,1)} async-done(((bf16[576,1024]{1,0:T(8,128)(2,1)}), bf16[144,1024]{1,0:T(8,128)(2,1)}) %reduce-scatter.5.cloned.1.call-update) | async-done | bytes 294928 | tf_op jit(solution)/shard_map/reduce_scatter | solution.py:115
  303.0 3.1 convolution_convert_fusion
  307.2 3.2 %fusion.38 = f32[576,512]{1,0:T(8,128)} fusion(bf16[1024,512]{1,0:T(8,128)(2,1)} %param.29, bf16[576,512]{1,0:T(8,128)(2,1)} %reshape.150, bf16[576,512]{1,0:T(8,128)(2,1)S(1)} %copy-done.7), kind=kOutput, calls=%fused_computation.63 | convolution fusion | flops 606339072 | bytes 3407872 | tf_op jit(solution)/shard_map/dot_general | solution.py:123
  (72 shorter events, 20.1 us)
Async XLA Ops:
  6.5 55.8 %copy-start = (bf16[2048,512]{1,0:T(8,128)(2,1)S(1)}, bf16[2048,512]{1,0:T(8,128)(2,1)}, u32[]{:S(2)}) copy-start(bf16[2048,512]{1,0:T(8,128)(2,1)} %param.22) | copy-start | bytes 6291460
  6.5 3.2 copy-start.2
  6.5 101.3 %all-gather.6.cloned.1.call-start = ((), (), s32[]{:S(2)}) async-start(), calls=%async_computation.2 | async-start | bytes 1474560 | tf_op jit(solution)/shard_map/all_gather | solution.py:103
  9.9 0.8 copy-start.6
  11.4 9.4 %collective-permute-start = (bf16[144,512]{1,0:T(8,128)(2,1)}, bf16[144,512]{1,0:T(8,128)(2,1)S(1)}, u32[]{:S(2)}, u32[]{:S(2)}) collective-permute-start(bf16[144,512]{1,0:T(8,128)(2,1)} %slice.58), channel_id=1, source_target_pairs={{0,31},{1,0},{2,1},{3,2},{4,3},{5,4},{6,5},{7,6},{8,7},{9,8},{10,9... | collective-permute-start | bytes 442376 | tf_op jit(solution)/shard_map/ppermute | solution.py:15
  32.2 4.5 %copy-start.3 = (bf16[8,576,192]{2,1,0:T(8,128)(2,1)S(1)}, bf16[8,576,192]{2,1,0:T(8,128)(2,1)}, u32[]{:S(2)}) copy-start(bf16[8,576,192]{2,1,0:T(8,128)(2,1)} %copy.26) | copy-start | bytes 5308420
  51.7 8.4 %collective-permute-start.1 = (bf16[144,512]{1,0:T(8,128)(2,1)S(1)}, bf16[144,512]{1,0:T(8,128)(2,1)S(1)}, u32[]{:S(2)}, u32[]{:S(2)}) collective-permute-start(bf16[144,512]{1,0:T(8,128)(2,1)S(1)} %slice.104), channel_id=1, source_target_pairs={{0,1},{1,2},{2,3},{3,4},{4,5},{5,6},{6,7},{7,8},{8,9},{9,10},{10,1... | collective-permute-start | bytes 442376 | tf_op jit(solution)/shard_map/ppermute | solution.py:15
  61.3 1.0 copy-start.5
  78.8 5.1 %copy-start.9 = (s32[4]{0:T(128)S(1)}, s32[4]{0:T(128)}, u32[]{:S(2)}) copy-start(s32[4]{0:T(128)} %param.18) | copy-start | bytes 52
  78.8 5.2 %copy-start.8 = (bf16[256,128]{1,0:T(8,128)(2,1)S(1)}, bf16[256,128]{1,0:T(8,128)(2,1)}, u32[]{:S(2)}) copy-start(bf16[256,128]{1,0:T(8,128)(2,1)} %param.25) | copy-start | bytes 196612
  83.1 51.7 %all-gather.8.cloned.1.call-start = ((), (), s32[]{:S(2)}) async-start(), calls=%async_computation.3 | async-start | bytes 1769472 | tf_op jit(solution)/shard_map/all_gather | solution.py:98
  83.8 89.2 %reduce-scatter.3.cloned.1.call-start = ((), (), s32[]{:S(2)}) async-start(), calls=%async_computation.4 | async-start | bytes 1474560 | tf_op jit(solution)/shard_map/reduce_scatter | solution.py:108
  145.0 58.6 %all-gather.12.cloned.1.call-start = ((), (), s32[]{:S(2)}) async-start(), calls=%async_computation.6 | async-start | bytes 2359296 | tf_op jit(solution)/shard_map/all_gather | solution.py:100
  145.6 89.5 %all-gather.14.cloned.1.call-start = ((), (), s32[]{:S(2)}) async-start(), calls=%async_computation.7 | async-start | bytes 2359296 | tf_op jit(solution)/shard_map/all_gather | solution.py:101
  146.2 117.3 %all-gather.10.cloned.1.call-start = ((), (), s32[]{:S(2)}) async-start(), calls=%async_computation.5 | async-start | bytes 1474560 | tf_op jit(solution)/shard_map/all_gather | solution.py:112
  177.2 125.8 %copy-start.4 = (bf16[144,1024]{1,0:T(8,128)(2,1)S(1)}, bf16[144,1024]{1,0:T(8,128)(2,1)}, u32[]{:S(2)}) copy-start(bf16[144,1024]{1,0:T(8,128)(2,1)} %reduce-scatter.3.cloned.1.call-done) | copy-start | bytes 884740
  177.2 125.8 %reduce-scatter.5.cloned.1.call-start = ((), (), s32[]{:S(2)}) async-start(), calls=%async_computation.8 | async-start | bytes 1474560 | tf_op jit(solution)/shard_map/reduce_scatter | solution.py:115
  274.1 33.1 %copy-start.7 = (bf16[576,512]{1,0:T(8,128)(2,1)S(1)}, bf16[576,512]{1,0:T(8,128)(2,1)}, u32[]{:S(2)}) copy-start(bf16[576,512]{1,0:T(8,128)(2,1)} %get-tuple-element.19) | copy-start | bytes 1769476
  306.1 4.4 %copy-start.1 = (bf16[2048,512]{1,0:T(8,128)(2,1)S(1)}, bf16[2048,512]{1,0:T(8,128)(2,1)}, u32[]{:S(2)}) copy-start(bf16[2048,512]{1,0:T(8,128)(2,1)} %param.22) | copy-start | bytes 6291460
Sparse Core Ops, SparseCore 0:
  83.2 24.5 all-gather.5
  109.4 25.2 all-gather.7
  145.2 27.8 reduce-scatter.2
  174.5 29.1 all-gather.11
  205.1 29.9 all-gather.13
  236.8 26.5 all-gather.9
  274.2 28.6 reduce-scatter.4
where the time goes:
time: 324 us; the launch traced here: 318 us
  waiting for transfers between devices  189 us (58%)
  matrix products  51 us (16%)
  local copies, waits for them, and re-layouts  23.7 us (7%)
  other arithmetic  17.6 us (5%)
  between operations  14.9 us (5%)
  blocking collectives  14 us (4%)
  starting transfers between devices  7.4 us (2%)
    all_gather x1, waiting for transfers between devices, body(): lax.all_gather(weight_parts[3], 'region', axis=1, tiled=True)  31.5 us
    reduce_scatter x1, waiting for transfers between devices, body(): lax.psum_scatter(mlp_terms.astype(jnp.bfloat16), 'head', scatter_dimensio...  28.9 us
    all_gather x1, waiting for transfers between devices, body(): mid_gathered = lax.all_gather(mid_norm, 'head', axis=0, tiled=True)  28.3 us
    all_gather x1, waiting for transfers between devices, body(): lax.all_gather(weight_parts[0], 'region', axis=0, tiled=True)  26.9 us
    reduce_scatter x1, waiting for transfers between devices, body(): lax.psum_scatter(partial_value.astype(jnp.bfloat16), 'head', scatter_dime...  26.8 us
    all_gather x1, waiting for transfers between devices, body(): lax.all_gather(weight_parts[2], 'region', axis=0, tiled=True)  26.2 us
    dot_general x1, matrix products, body(): jnp.dot(fine_hidden, fine_down, preferred_element_type=jnp.float32)  14.1 us
    all_gather x1, blocking collectives, body(): lax.all_gather(weight_parts[1], 'region', axis=1, tiled=True)  14 us
  transfers between devices with their start and end apart: 9, of which 9 were waited for; matrix products, arithmetic and copies ran while one was open for 2% of the time, Pallas kernels for 0%

commit v1 on v0

v1 whole, which is shorter than its diff:
```python
import functools

import jax
import jax.numpy as jnp
from jax import lax
from jax.experimental import pallas as pl
from jax.experimental.pallas import tpu as pltpu
from jax.sharding import PartitionSpec as P

C = 512
HD = 64
HF = 8
WIN = 144
HEADS = HF
MESH = pl.DeviceIdType.MESH
F32 = jnp.float32
BF16 = jnp.bfloat16


def norm(values):
    average = jnp.mean(values, axis=-1, keepdims=True)
    centred = values - average
    spread = jnp.mean(centred * centred, axis=-1, keepdims=True)
    return centred * lax.rsqrt(spread + 1e-05)


def gelu(values):
    return 0.5 * values * (1.0 + lax.erf(values * (0.5**0.5)))


def dot(left, right):
    return jnp.dot(left, right, preferred_element_type=F32)


def flip(index, mask):
    result = index
    bit = 1
    while bit <= mask:
        if mask & bit:
            result = result + (1 - 2 * ((index // bit) % 2)) * bit
        bit *= 2
    return result


def attend(packed, head_count, count):
    blended = []
    for head in range(head_count):
        base = head * 3 * HD
        query = packed[:, base : base + HD]
        key = packed[:, base + HD : base + 2 * HD]
        value = packed[:, base + 2 * HD : base + 3 * HD]
        scores = lax.dot_general(
            query, key, (((1,), (1,)), ((), ())), preferred_element_type=F32
        ) * (HD**-0.5)
        if count is not None:
            place = lax.broadcasted_iota(jnp.int32, scores.shape, 1)
            scores = jnp.where(place < count, scores, -1e30)
        raised = jnp.exp(scores - jnp.max(scores, axis=-1, keepdims=True))
        weights = (raised / jnp.sum(raised, axis=-1, keepdims=True)).astype(BF16)
        blended.append(dot(weights, value).astype(BF16))
    return blended


def kernel(
    region_count, head_count,
    shift, counts, tokens, w_qkv, w_proj, w_up, w_down, w_merge,
    c_qkv, c_proj, c_up, c_down, w_expand, w_out,
    out,
    v_qkv, v_proj, v_up, v_down, v_merge, v_expand, v_out,
    g_qkv, g_proj, g_up, g_down,
    extended, rolled, packed, blended, fine, fine_bf, hidden, grouped,
    coarse, shared, c_packed, c_blended, sent_blend, got_blend, mid, c_hidden, parts, got_parts, spread, lanes,
    local_sem, halo_send, halo_recv, own_sem, z_send, w_recv, p_send, q_send, q_recv,
    a_send, a_recv, b_send, b_recv, m_send, m_recv, r_send, r_recv,
):
    region, head = lax.axis_index("region"), lax.axis_index("head")
    chips = region_count // 2
    chip, core = region // 2, region % 2
    rows = tokens.shape[0]
    blocks = rows // WIN
    flat = region * head_count + head
    total = region_count * head_count
    before, after = (flat + total - 1) % total, (flat + 1) % total
    before = (before // head_count, before % head_count)
    after = (after // head_count, after % head_count)
    partner = (chip * 2 + 1 - core, head)
    column = [(((chip + s) % chips) * 2 + core, head) for s in range(chips)]
    plane = [(region, flip(head, k)) for k in range(head_count)]

    barrier = pltpu.get_barrier_semaphore()
    greeted = [before, after, partner] + column[1:] + plane[1:]
    for device in greeted:
        pl.semaphore_signal(barrier, inc=1, device_id=device, device_id_type=MESH)

    own = []
    for at, (source, target) in enumerate(
        [(w_qkv, v_qkv), (w_proj, v_proj), (w_up, v_up), (w_down, v_down), (w_merge, v_merge),
         (w_expand, v_expand), (w_out, v_out)]
    ):
        copy = pltpu.make_async_copy(source, target, local_sem.at[at])
        copy.start()
        own.append(copy)

    shards = [c_proj, c_qkv, c_up, c_down]

    def slot(which, owner):
        if which == 0:
            return g_proj.at[head, owner]
        if which == 1:
            return g_qkv.at[pl.ds(owner * c_qkv.shape[0], c_qkv.shape[0])]
        if which == 2:
            return g_up.at[pl.ds(owner * c_up.shape[0], c_up.shape[0])]
        return g_down.at[owner]

    own_shards = []
    for which in range(4):
        copy = pltpu.make_async_copy(shards[which], slot(which, region), own_sem.at[which])
        copy.start()
        own_shards.append(copy)

    def remote(source, target, send, recv, device):
        return pltpu.make_async_remote_copy(
            src_ref=source, dst_ref=target, send_sem=send, recv_sem=recv,
            device_id=device, device_id_type=MESH,
        )

    extended[WIN : WIN + rows, :] = norm(tokens[...]).astype(BF16)
    pl.semaphore_wait(barrier, len(greeted))

    halo_left = remote(extended.at[pl.ds(WIN, WIN)], extended.at[pl.ds(WIN + rows, WIN)],
                       halo_send.at[0], halo_recv.at[0], before)
    halo_right = remote(extended.at[pl.ds(rows, WIN)], extended.at[pl.ds(0, WIN)],
                        halo_send.at[1], halo_recv.at[1], after)
    halo_left.start()
    halo_right.start()

    column_sends = []
    for which in range(4):
        for s in range(1, chips):
            copy = remote(shards[which], slot(which, region), z_send.at[which, s],
                          w_recv.at[which, region], column[s])
            copy.start()
            column_sends.append(copy)

    partner_sends = []

    def pass_on(which):
        for s in range(chips):
            owner = ((chip + s) % chips) * 2 + core
            if s == 0:
                own_shards[which].wait()
            else:
                remote(shards[which], slot(which, owner), z_send.at[which, s],
                       w_recv.at[which, owner], column[s]).wait_recv()
            copy = remote(slot(which, owner), slot(which, owner), p_send.at[which, s],
                          w_recv.at[which, owner], partner)
            copy.start()
            partner_sends.append(copy)

    def take_over(which):
        for s in range(chips):
            owner = ((chip + s) % chips) * 2 + 1 - core
            remote(slot(which, owner), slot(which, owner), p_send.at[which, s],
                   w_recv.at[which, owner], partner).wait_recv()

    offset = shift[0]
    at_row = lax.broadcasted_iota(jnp.int32, (WIN, 2 * WIN), 0)
    at_column = lax.broadcasted_iota(jnp.int32, (WIN, 2 * WIN), 1)
    forth = (at_column == at_row + offset).astype(F32).astype(BF16)
    back = (at_column == at_row + (WIN - offset)).astype(F32).astype(BF16)
    halo_left.wait()
    halo_right.wait()
    for j in range(blocks + 1):
        rolled[j * WIN : (j + 1) * WIN, :] = dot(
            forth, extended[j * WIN : (j + 2) * WIN, :]
        ).astype(BF16)
    own[0].wait()

    def project(i, carry):
        at = pl.ds(pl.multiple_of(i * 256, 256), 256)
        packed[:, at] = dot(rolled[...], v_qkv[:, at]).astype(BF16)
        return carry

    lax.fori_loop(0, packed.shape[1] // 256, project, 0)

    def window(j, carry):
        at = pl.ds(pl.multiple_of(j * WIN, WIN), WIN)
        for half in range(2):
            width = packed.shape[1] // 2
            parts_of = attend(packed[at, half * width : (half + 1) * width], HEADS // 2, None)
            blended[at, half * (C // 2) : (half + 1) * (C // 2)] = jnp.concatenate(parts_of, axis=1)
        return carry

    lax.fori_loop(0, blocks + 1, window, 0)
    own[1].wait()
    for j in range(blocks):
        at = slice(j * WIN, (j + 1) * WIN)
        rolled[at, :] = dot(back, blended[j * WIN : (j + 2) * WIN, :]).astype(BF16)
    fine[...] = tokens[...] + dot(rolled[:rows, :], v_proj[...])
    rolled[:rows, :] = norm(fine[...]).astype(BF16)

    pass_on(0)
    own[2].wait()

    def fine_hidden(i, carry):
        at = pl.ds(pl.multiple_of(i * 256, 256), 256)
        hidden[:, at] = gelu(dot(rolled[:rows, :], v_up[:, at])).astype(BF16)
        return carry

    chunks = hidden.shape[1] // 256
    lax.fori_loop(0, chunks, fine_hidden, 0)
    take_over(0)
    quarter = []
    for k in range(1, head_count):
        copy = remote(g_proj.at[head], g_proj.at[head], q_send.at[k], q_recv.at[k], plane[k])
        copy.start()
        quarter.append(copy)
    own[3].wait()

    def fine_sum(i, carry):
        at = pl.ds(pl.multiple_of(i * 256, 256), 256)
        fine[:, at] += dot(hidden[...], v_down[:, at])
        return carry

    lax.fori_loop(0, C // 256, fine_sum, 0)
    pass_on(1)

    group = w_merge.shape[0] // C
    cells = rows // group
    own[4].wait()
    members = []
    for c in range(C // 128):
        lanes[c] = fine[:, c * 128 : (c + 1) * 128]
    for k in range(group):
        pieces = [lanes[c, pl.ds(k, cells, stride=group), :] for c in range(C // 128)]
        member = jnp.concatenate(pieces, axis=1)
        fine_bf[k * cells : (k + 1) * cells, :] = member.astype(BF16)
        members.append(member)
    merged = jnp.concatenate(members, axis=1)
    grouped[...] = norm(merged).astype(BF16)
    width = coarse.shape[1]

    def merge(i, carry):
        at = pl.ds(pl.multiple_of(i * 256, 256), 256)
        coarse[:, at] = dot(grouped[...], v_merge[:, at])
        return carry

    lax.fori_loop(0, width // 256, merge, 0)
    shared[head] = norm(coarse[...]).astype(BF16)
    gathers = []
    for k in range(1, head_count):
        copy = remote(shared.at[head], shared.at[head], a_send.at[k], a_recv.at[k], plane[k])
        copy.start()
        gathers.append(copy)
    take_over(1)

    blends = []
    heads_here = g_qkv.shape[1] // (3 * HD)
    for k in range(head_count):
        target = plane[k][1]
        if k > 0:
            gathers[k - 1].wait_recv()
        c_packed[...] = dot(shared[target], g_qkv[...]).astype(BF16)
        parts_of = attend(c_packed[...], heads_here, counts[target])
        if k == 0:
            got_blend[head] = jnp.concatenate(parts_of, axis=1)
        else:
            sent_blend[k] = jnp.concatenate(parts_of, axis=1)
            copy = remote(sent_blend.at[k], got_blend.at[head], b_send.at[k], b_recv.at[k], plane[k])
            copy.start()
            blends.append(copy)
    pass_on(2)
    for copy in quarter:
        copy.wait_recv()
    for copy in blends:
        copy.wait_recv()
    for r in range(region_count):
        w = g_proj.shape[3]
        total_of = dot(got_blend[0], g_proj[0, r])
        for h in range(1, head_count):
            total_of += dot(got_blend[h], g_proj[h, r])
        mid[:, r * w : (r + 1) * w] = coarse[:, r * w : (r + 1) * w] + total_of

    for copy in gathers:
        copy.wait_send()
    c_blended[head] = norm(mid[...]).astype(BF16)
    seconds = []
    for k in range(1, head_count):
        copy = remote(c_blended.at[head], c_blended.at[head], m_send.at[k], m_recv.at[k], plane[k])
        copy.start()
        seconds.append(copy)
    take_over(2)
    pass_on(3)

    returns = []
    for k in range(head_count):
        target = plane[k][1]
        if k > 0:
            seconds[k - 1].wait_recv()

        def coarse_hidden(i, carry):
            at = pl.ds(pl.multiple_of(i * 256, 256), 256)
            c_hidden[:, at] = gelu(dot(c_blended[target], g_up[:, at])).astype(BF16)
            return carry

        lax.fori_loop(0, c_hidden.shape[1] // 256, coarse_hidden, 0)
        if k == 0:
            take_over(3)
        w = g_down.shape[2]
        for r in range(0, region_count, 2):
            pair = jnp.concatenate([g_down[r], g_down[r + 1]], axis=1)
            term = dot(c_hidden[...], pair)
            if k == 0:
                mid[:, r * w : (r + 2) * w] += term
            else:
                parts[k, :, r * w : (r + 2) * w] = term.astype(BF16)
        if k > 0:
            copy = remote(parts.at[k], got_parts.at[k], r_send.at[k], r_recv.at[k], plane[k])
            copy.start()
            returns.append(copy)
    own[5].wait()
    own[6].wait()
    for copy in returns:
        copy.wait_recv()
    result = mid[...]
    for k in range(1, head_count):
        result += got_parts[k].astype(F32)
    grouped[:, :width] = result.astype(BF16)
    for k in range(group):
        spread[k * cells : (k + 1) * cells, :] = dot(
            grouped[:, :width], v_expand[:, k * C : (k + 1) * C]
        ).astype(BF16)
    for c in range(C // 128):
        at = slice(c * 128, (c + 1) * 128)
        value = dot(fine_bf[...], v_out[:C, at]) + dot(spread[...], v_out[C:, at])
        for k in range(group):
            lanes[c, pl.ds(k, cells, stride=group), :] = value[k * cells : (k + 1) * cells, :]
        out[:, at] = lanes[c]

    for copy in column_sends + partner_sends + quarter + blends + seconds + returns:
        copy.wait_send()


def body(region_count, head_count, tokens, shift, counts, *weights):
    rows = tokens.shape[0]
    w_qkv, w_proj, w_up, w_down, w_merge, c_qkv, c_proj, c_up, c_down, w_expand, w_out = weights
    width = w_merge.shape[1]
    group = w_merge.shape[0] // C
    cells = rows // group
    vmem = pltpu.VMEM
    any_spec = pl.BlockSpec(memory_space=pl.ANY)
    dma = pltpu.SemaphoreType.DMA
    chips = region_count // 2
    mine = c_proj.shape[0]
    scratch = [vmem(w.shape, BF16) for w in (w_qkv, w_proj, w_up, w_down, w_merge, w_expand, w_out)]
    scratch += [
        vmem((width, c_qkv.shape[1]), BF16),
        vmem((head_count, region_count) + c_proj.shape, BF16),
        vmem((width, c_up.shape[1]), BF16),
        vmem((region_count,) + c_down.shape, BF16),
        vmem((rows + 2 * WIN, C), BF16),
        vmem((rows + WIN, C), BF16),
        vmem((rows + WIN, w_qkv.shape[1]), BF16),
        vmem((rows + WIN, C), BF16),
        vmem((rows, C), F32),
        vmem((rows, C), BF16),
        vmem((rows, w_up.shape[1]), BF16),
        vmem((cells, group * C), BF16),
        vmem((cells, width), F32),
        vmem((head_count, cells, width), BF16),
        vmem((cells, c_qkv.shape[1]), BF16),
        vmem((head_count, cells, width), BF16),
        vmem((head_count, cells, mine), BF16),
        vmem((head_count, cells, mine), BF16),
        vmem((cells, width), F32),
        vmem((cells, c_up.shape[1]), BF16),
        vmem((head_count, cells, width), BF16),
        vmem((head_count, cells, width), BF16),
        vmem((rows, C), BF16),
        vmem((C // 128, rows, 128), F32),
        dma((7,)), dma((2,)), dma((2,)), dma((4,)), dma((4, chips)), dma((4, region_count)), dma((4, chips)),
    ]
    scratch += [dma((head_count,)) for _ in range(10)]
    return pl.pallas_call(
        functools.partial(kernel, region_count, head_count),
        out_shape=jax.ShapeDtypeStruct((rows, C), F32),
        in_specs=[pl.BlockSpec(memory_space=pltpu.SMEM)] * 2
        + [pl.BlockSpec(memory_space=pltpu.VMEM)] + [any_spec] * 11,
        out_specs=pl.BlockSpec(memory_space=pltpu.VMEM),
        scratch_shapes=scratch,
        compiler_params=pltpu.CompilerParams(
            collective_id=0, has_side_effects=True, vmem_limit_bytes=60 * 1024 * 1024
        ),
    )(shift, counts, tokens, *weights)


def solution(mesh):
    in_specs = (
        P(("region", "head"), None), P(), P("region"), P(), P(), P(), P(), P(),
        P("region", "head"), P("head", "region"), P("region", "head"), P("head", "region"), P(), P(),
    )
    out_specs = P(("region", "head"), None)
    run = functools.partial(body, mesh.shape["region"], mesh.shape["head"])
    return jax.shard_map(run, mesh=mesh, in_specs=in_specs, out_specs=out_specs, check_vma=False)
```

time: 324 us -> 108 us (0.33)
  the two profiles are of different devices: /device:TPU:0 before, /device:TPU:8 now
where the time goes in v1:
time: 108 us; the launch traced here: 107 us
  Pallas kernels  104 us (96%)
  local copies, waits for them, and re-layouts  2.36 us (2%)
    pallas_call x1, Pallas kernels, body(): pl.pallas_call(functools.partial(kernel, region_count, head_count), out_s...  104 us
    unnamed x1, local copies, waits for them, and re-layouts  2.36 us

profile of v1, /device:TPU:8, one launch (start us, length us, event | category | flops | bytes accessed | tf_op | source)
XLA Modules:
  0.0 107.4 jit_solution(7059476848916988304)
XLA Ops:
  0.7 104.4 %shard_map.136 = f32[576,512]{1,0:T(8,128)} custom-call(s32[1]{0:T(128)S(6)} %copy.16.shift, s32[4]{0:T(128)} %counts.1, f32[576,512]{1,0:T(8,128)} %tokens.1, bf16[512,1536]{1,0:T(8,128)(2,1)} %w_qkv.1, bf16[512,512]{1,0:T(8,128)(2,1)} %w_proj.1, bf16[512,2048]{1,0:T(8,128)(2,1)} %w_up.1, bf16[2048,512]{1,0:T(8,128)(2,1)} %w_down.1, ...), custom_call_target="tpu_custom_call" | custom-call | tf_op jit(solution)/shard_map/pallas_call | solution.py:384
  105.0 2.4 %copy.17 = f32[576,512]{1,0:T(8,128)} copy(f32[576,512]{1,0:T(8,128)} %shard_map.136) | data formatting | bytes 2359296

commit v2 on v1

--- a/solution.py
+++ b/solution.py
@@ -70,7 +70,7 @@
     g_qkv, g_proj, g_up, g_down,
     extended, rolled, packed, blended, fine, fine_bf, hidden, grouped,
     coarse, shared, c_packed, c_blended, sent_blend, got_blend, mid, c_hidden, parts, got_parts, spread, lanes,
-    local_sem, halo_send, halo_recv, own_sem, z_send, w_recv, p_send, q_send, q_recv,
+    local_sem, halo_send, halo_recv, own_sem, z_send, w_recv, p_send, q_send, q_recv, x_send, x_recv,
     a_send, a_recv, b_send, b_recv, m_send, m_recv, r_send, r_recv,
 ):
     region, head = lax.axis_index("region"), lax.axis_index("head")
@@ -163,6 +163,38 @@
             remote(slot(which, owner), slot(which, owner), p_send.at[which, s],
                    w_recv.at[which, owner], partner).wait_recv()
 
+    relay = head_count == 4
+
+    def gather(buffer, send, recv):
+        copies = []
+        for k in range(1, 3 if relay else head_count):
+            piece = buffer.at[head]
+            copy = remote(piece, piece, send.at[k], recv.at[k], plane[k])
+            copy.start()
+            copies.append(copy)
+        return copies
+
+    def far_half(buffer, mask, i, send, recv, device):
+        half = buffer.shape[2] // 2
+        piece = buffer.at[flip(head, mask), :, pl.ds(i * half, half)]
+        return remote(piece, piece, send.at[3 * i], recv.at[3 * i], device)
+
+    def hand_on(buffer, send, recv, copies):
+        if not relay:
+            return
+        for i, (came, goes) in enumerate(((1, 2), (2, 1))):
+            copies[came - 1].wait_recv()
+            copy = far_half(buffer, came, i, send, recv, plane[goes])
+            copy.start()
+            copies.append(copy)
+
+    def arrived(buffer, k, send, recv, copies):
+        if not relay:
+            copies[k - 1].wait_recv()
+        elif k == 3:
+            for i, came in enumerate((2, 1)):
+                far_half(buffer, 3, i, send, recv, plane[came]).wait_recv()
+
     offset = shift[0]
     at_row = lax.broadcasted_iota(jnp.int32, (WIN, 2 * WIN), 0)
     at_column = lax.broadcasted_iota(jnp.int32, (WIN, 2 * WIN), 1)
@@ -182,6 +214,15 @@
         return carry
 
     lax.fori_loop(0, packed.shape[1] // 256, project, 0)
+    pass_on(0)
+    quarter = []
+    for s in range(chips):
+        owner = ((chip + s) % chips) * 2 + core
+        for k in range(1, head_count):
+            piece = g_proj.at[head, owner]
+            copy = remote(piece, piece, q_send.at[k, s], q_recv.at[k, s], plane[k])
+            copy.start()
+            quarter.append(copy)
 
     def window(j, carry):
         at = pl.ds(pl.multiple_of(j * WIN, WIN), WIN)
@@ -199,7 +240,14 @@
     fine[...] = tokens[...] + dot(rolled[:rows, :], v_proj[...])
     rolled[:rows, :] = norm(fine[...]).astype(BF16)
 
-    pass_on(0)
+    for s in range(chips):
+        owner = ((chip + s) % chips) * 2 + core
+        for k in range(1, head_count):
+            piece = g_proj.at[plane[k][1], owner]
+            remote(piece, piece, q_send.at[k, s], q_recv.at[k, s], plane[k]).wait_recv()
+            copy = remote(piece, piece, x_send.at[k, s], x_recv.at[k, s], partner)
+            copy.start()
+            partner_sends.append(copy)
     own[2].wait()
 
     def fine_hidden(i, carry):
@@ -209,12 +257,6 @@
 
     chunks = hidden.shape[1] // 256
     lax.fori_loop(0, chunks, fine_hidden, 0)
-    take_over(0)
-    quarter = []
-    for k in range(1, head_count):
-        copy = remote(g_proj.at[head], g_proj.at[head], q_send.at[k], q_recv.at[k], plane[k])
-        copy.start()
-        quarter.append(copy)
     own[3].wait()
 
     def fine_sum(i, carry):
@@ -247,11 +289,7 @@
 
     lax.fori_loop(0, width // 256, merge, 0)
     shared[head] = norm(coarse[...]).astype(BF16)
-    gathers = []
-    for k in range(1, head_count):
-        copy = remote(shared.at[head], shared.at[head], a_send.at[k], a_recv.at[k], plane[k])
-        copy.start()
-        gathers.append(copy)
+    gathers = gather(shared, a_send, a_recv)
     take_over(1)
 
     blends = []
@@ -259,19 +297,24 @@
     for k in range(head_count):
         target = plane[k][1]
         if k > 0:
-            gathers[k - 1].wait_recv()
+            arrived(shared, k, a_send, a_recv, gathers)
         c_packed[...] = dot(shared[target], g_qkv[...]).astype(BF16)
         parts_of = attend(c_packed[...], heads_here, counts[target])
         if k == 0:
             got_blend[head] = jnp.concatenate(parts_of, axis=1)
+            hand_on(shared, a_send, a_recv, gathers)
         else:
             sent_blend[k] = jnp.concatenate(parts_of, axis=1)
             copy = remote(sent_blend.at[k], got_blend.at[head], b_send.at[k], b_recv.at[k], plane[k])
             copy.start()
             blends.append(copy)
     pass_on(2)
-    for copy in quarter:
-        copy.wait_recv()
+    take_over(0)
+    for s in range(chips):
+        owner = ((chip + s) % chips) * 2 + 1 - core
+        for k in range(1, head_count):
+            piece = g_proj.at[plane[k][1], owner]
+            remote(piece, piece, x_send.at[k, s], x_recv.at[k, s], partner).wait_recv()
     for copy in blends:
         copy.wait_recv()
     for r in range(region_count):
@@ -281,14 +324,8 @@
             total_of += dot(got_blend[h], g_proj[h, r])
         mid[:, r * w : (r + 1) * w] = coarse[:, r * w : (r + 1) * w] + total_of
 
-    for copy in gathers:
-        copy.wait_send()
     c_blended[head] = norm(mid[...]).astype(BF16)
-    seconds = []
-    for k in range(1, head_count):
-        copy = remote(c_blended.at[head], c_blended.at[head], m_send.at[k], m_recv.at[k], plane[k])
-        copy.start()
-        seconds.append(copy)
+    seconds = gather(c_blended, m_send, m_recv)
     take_over(2)
     pass_on(3)
 
@@ -296,7 +333,7 @@
     for k in range(head_count):
         target = plane[k][1]
         if k > 0:
-            seconds[k - 1].wait_recv()
+            arrived(c_blended, k, m_send, m_recv, seconds)
 
         def coarse_hidden(i, carry):
             at = pl.ds(pl.multiple_of(i * 256, 256), 256)
@@ -305,6 +342,7 @@
 
         lax.fori_loop(0, c_hidden.shape[1] // 256, coarse_hidden, 0)
         if k == 0:
+            hand_on(c_blended, m_send, m_recv, seconds)
             take_over(3)
         w = g_down.shape[2]
         for r in range(0, region_count, 2):
@@ -337,7 +375,7 @@
             lanes[c, pl.ds(k, cells, stride=group), :] = value[k * cells : (k + 1) * cells, :]
         out[:, at] = lanes[c]
 
-    for copy in column_sends + partner_sends + quarter + blends + seconds + returns:
+    for copy in column_sends + partner_sends + quarter + gathers + blends + seconds + returns:
         copy.wait_send()
 
 
@@ -380,7 +418,8 @@
         vmem((C // 128, rows, 128), F32),
         dma((7,)), dma((2,)), dma((2,)), dma((4,)), dma((4, chips)), dma((4, region_count)), dma((4, chips)),
     ]
-    scratch += [dma((head_count,)) for _ in range(10)]
+    scratch += [dma((head_count, chips)) for _ in range(4)]
+    scratch += [dma((head_count,)) for _ in range(8)]
     return pl.pallas_call(
         functools.partial(kernel, region_count, head_count),
         out_shape=jax.ShapeDtypeStruct((rows, C), F32),

time: 108 us -> 106 us (0.981)
    pallas_call x1, Pallas kernels: 104 us -> 103 us  [body(): pl.pallas_call(functools.partial(kernel, region_count, head_count), out_s...]
where the time goes in v2:
time: 106 us
  Pallas kernels  103 us (97%)
  local copies, waits for them, and re-layouts  2.36 us (2%)
    pallas_call x1, Pallas kernels, body(): pl.pallas_call(functools.partial(kernel, region_count, head_count), out_s...  103 us
    unnamed x1, local copies, waits for them, and re-layouts  2.36 us

profile of v2, /device:TPU:8, one launch (start us, length us, event | category | flops | bytes accessed | tf_op | source)
XLA Modules:
  0.0 105.6 jit_solution(157955464198786629)
XLA Ops:
  0.7 102.6 %shard_map.136 = f32[576,512]{1,0:T(8,128)} custom-call(s32[1]{0:T(128)S(6)} %copy.16.shift, s32[4]{0:T(128)} %counts.1, f32[576,512]{1,0:T(8,128)} %tokens.1, bf16[512,1536]{1,0:T(8,128)(2,1)} %w_qkv.1, bf16[512,512]{1,0:T(8,128)(2,1)} %w_proj.1, bf16[512,2048]{1,0:T(8,128)(2,1)} %w_up.1, bf16[2048,512]{1,0:T(8,128)(2,1)} %w_down.1, ...), custom_call_target="tpu_custom_call" | custom-call | tf_op jit(solution)/shard_map/pallas_call | solution.py:423
  103.2 2.4 %copy.17 = f32[576,512]{1,0:T(8,128)} copy(f32[576,512]{1,0:T(8,128)} %shard_map.136) | data formatting | bytes 2359296
